TPU v7x, 32 devices: a whole 2x2x4 slice. The times are simulated.
32 devices in a mesh: gx: 4 (over x, core), gy: 8 (over z, y).
Axes of the slice: x: 2, y: 2, z: 4, core: 2. Of those that a mesh axis runs over, the one named last changes fastest.
Arguments:
- tokens: bfloat16 [2740, 1024], P('gx', 'gy'), may hold values from -64 to 64
- cotangent: bfloat16 [2740, 1024], P('gx', 'gy'), may hold values from -6 to 6
- norm1_gain: float32 [1024], P('gy'), may hold values from 0.1 to 1.9
- norm1_shift: float32 [1024], P('gy'), may hold values from -1.5 to 1.5
- qkv_weight: bfloat16 [1024, 3072], P('gx', 'gy'), may hold values from -4 to 4
- qv_bias: float32 [2048], P('gy'), may hold values from -2.5 to 2.5
- proj_weight: bfloat16 [1024, 1024], P('gx', 'gy'), may hold values from -1.5 to 1.5
- proj_bias: float32 [1024], P('gy'), may hold values from -1.5 to 1.5
- scale_attn: float32 [1024], P('gy'), may hold values from 0.3 to 1.5
- norm2_gain: float32 [1024], P('gy'), may hold values from 0.1 to 1.9
- norm2_shift: float32 [1024], P('gy'), may hold values from -1.5 to 1.5
- fc1_weight: bfloat16 [1024, 4096], P('gx', 'gy'), may hold values from -0.1875 to 0.1875
- fc1_bias: float32 [4096], P('gy'), may hold values from -2.5 to 2.5
- fc2_weight: bfloat16 [4096, 1024], P('gx', 'gy'), may hold values from -0.09375 to 0.09375
- fc2_bias: float32 [1024], P('gy'), may hold values from -1.5 to 1.5
- scale_mlp: float32 [1024], P('gy'), may hold values from 0.3 to 1.5
Outputs:
- output: float32 [2740, 1024], P('gx', 'gy')
- grad_tokens: float32 [2740, 1024], P('gx', 'gy')
- grad_norm1_gain: float32 [1024], P('gy')
- grad_norm1_shift: float32 [1024], P('gy')
- grad_qkv_weight: float32 [1024, 3072], P('gx', 'gy')
- grad_qv_bias: float32 [2048], P('gy')
- grad_proj_weight: float32 [1024, 1024], P('gx', 'gy')
- grad_proj_bias: float32 [1024], P('gy')
- grad_scale_attn: float32 [1024], P('gy')
- grad_norm2_gain: float32 [1024], P('gy')
- grad_norm2_shift: float32 [1024], P('gy')
- grad_fc1_weight: float32 [1024, 4096], P('gx', 'gy')
- grad_fc1_bias: float32 [4096], P('gy')
- grad_fc2_weight: float32 [4096, 1024], P('gx', 'gy')
- grad_fc2_bias: float32 [1024], P('gy')
- grad_scale_mlp: float32 [1024], P('gy')
All inputs are finite; a program needn't handle non-finite values.
Results may differ from a plain program's by a relative error of at most 0.012.
Values may be sent and summed in bfloat16 or wider, within the bound.
A program may use at most 128 MiB of HBM per device.

v0:
```python
import jax
import jax.numpy as jnp
from jax import lax
from jax.sharding import PartitionSpec as P

D = 1024
HD = 64
IMGS = 1
EPS = 1e-06
ROOT_HALF = 0.7071067811865476
INV_ROOT_TAU = 0.3989422804014327


def from_partner(block, axis, bit):
    count = lax.axis_size(axis)
    route = []
    for low in range(count):
        high = low | 1 << bit
        if high != low and high < count:
            route += [(low, high), (high, low)]
    return lax.ppermute(block, axis, route)


def normal_cdf(values):
    return 0.5 * (1.0 + jax.scipy.special.erf(values * ROOT_HALF))


def gelu_exact(values):
    return values * normal_cdf(values)


def gelu_slope(values):
    return normal_cdf(values) + values * jnp.exp(-0.5 * values * values) * INV_ROOT_TAU


def norm_forward(rows, gain, shift):
    totals, squares = lax.psum((jnp.sum(rows, axis=1), jnp.sum(rows * rows, axis=1)), "gy")
    row_mean = totals / D
    inv_std = lax.rsqrt(squares / D - row_mean * row_mean + EPS)[:, None]
    normed = (rows - row_mean[:, None]) * inv_std
    return (normed, inv_std, (normed * gain + shift).astype(jnp.bfloat16))


def norm_backward(grad_normed, normed, inv_std, gain):
    scaled = grad_normed * gain
    first, second = lax.psum((jnp.sum(scaled, axis=1), jnp.sum(scaled * normed, axis=1)), "gy")
    return inv_std * (scaled - first[:, None] / D - normed * (second[:, None] / D))


def project(inputs, weight):
    result = jnp.dot(
        lax.all_gather(inputs, "gy", axis=1, tiled=True), weight, preferred_element_type=jnp.float32
    )
    return (result, inputs)


def weight_grad(saved, grad_out):
    return jnp.einsum(
        "tk,tn->kn",
        lax.all_gather(saved, "gy", axis=1, tiled=True),
        grad_out,
        preferred_element_type=jnp.float32,
    )


def back_project(grad_out, weight):
    term = jnp.einsum("tn,kn->tk", grad_out, weight, preferred_element_type=jnp.float32)
    return lax.psum_scatter(term, "gy", scatter_dimension=1, tiled=True)


def on_device(
    tokens,
    cotangent,
    norm1_gain,
    norm1_shift,
    qkv_weight,
    qv_bias,
    proj_weight,
    proj_bias,
    scale_attn,
    norm2_gain,
    norm2_shift,
    fc1_weight,
    fc1_bias,
    fc2_weight,
    fc2_bias,
    scale_mlp,
):
    count = tokens.shape[0]
    half_len = count // IMGS
    heads_here = qkv_weight.shape[1] // (3 * HD)
    factor = HD ** (-0.5)
    full_qkv, full_proj, full_fc1, full_fc2 = (
        lax.all_gather(qkv_weight, "gx", axis=0, tiled=True),
        lax.all_gather(proj_weight, "gx", axis=0, tiled=True),
        lax.all_gather(fc1_weight, "gx", axis=0, tiled=True),
        lax.all_gather(fc2_weight, "gx", axis=0, tiled=True),
    )
    inputs = tokens.astype(jnp.float32)
    normed_one, inv_one, norm_one = norm_forward(inputs, norm1_gain, norm1_shift)
    mixed, saved_one = project(norm_one, full_qkv)
    mixed = mixed.reshape(count, heads_here, 3, HD)
    biases = qv_bias.reshape(heads_here, 2, HD)
    queries = (mixed[:, :, 0] + biases[:, 0]).astype(jnp.bfloat16)
    keys = mixed[:, :, 1].astype(jnp.bfloat16)
    values = (mixed[:, :, 2] + biases[:, 1]).astype(jnp.bfloat16)
    lower = lax.axis_index("gx") % 2 == 0
    pair_kv = jnp.concatenate([keys, values], axis=2).reshape(count, heads_here * 2 * HD)
    other_kv = from_partner(pair_kv, "gx", 0)
    first_kv = jnp.where(lower, pair_kv, other_kv)
    second_kv = jnp.where(lower, other_kv, pair_kv)
    image_shape = (IMGS, half_len, heads_here, 2 * HD)
    both_kv = jnp.concatenate(
        [first_kv.reshape(image_shape), second_kv.reshape(image_shape)], axis=1
    )
    key_all = both_kv[..., :HD]
    value_all = both_kv[..., HD:]
    query_img = queries.reshape(IMGS, half_len, heads_here, HD)
    scores = (
        jnp.einsum("iqhe,ikhe->ihqk", query_img, key_all, preferred_element_type=jnp.float32)
        * factor
    )
    row_max = jnp.max(scores, axis=3, keepdims=True)
    exponent = jnp.exp(scores - row_max)
    totals = jnp.sum(exponent, axis=3, keepdims=True)
    log_total = row_max + jnp.log(totals)
    probs = (exponent / totals).astype(jnp.bfloat16)
    attended_img = jnp.einsum(
        "ihqk,ikhe->iqhe", probs, value_all, preferred_element_type=jnp.float32
    ).astype(jnp.bfloat16)
    attended = attended_img.reshape(count, heads_here * HD)
    attn_out, saved_two = project(attended, full_proj)
    attn_out = attn_out + proj_bias
    middle = inputs + scale_attn * attn_out
    normed_two, inv_two, norm_two = norm_forward(middle, norm2_gain, norm2_shift)
    pre_act, saved_three = project(norm_two, full_fc1)
    pre_act = pre_act + fc1_bias
    hidden = gelu_exact(pre_act).astype(jnp.bfloat16)
    mlp_out, saved_four = project(hidden, full_fc2)
    mlp_out = mlp_out + fc2_bias
    output = middle + scale_mlp * mlp_out
    upstream = cotangent.astype(jnp.float32)
    grad_scale_mlp = jnp.sum(upstream * mlp_out, axis=0)
    grad_mlp = upstream * scale_mlp
    grad_fc2_bias = jnp.sum(grad_mlp, axis=0)
    grad_mlp_b = grad_mlp.astype(jnp.bfloat16)
    grad_fc2 = weight_grad(saved_four, grad_mlp_b)
    grad_hidden = back_project(grad_mlp_b, full_fc2)
    grad_pre = grad_hidden * gelu_slope(pre_act)
    grad_fc1_bias = jnp.sum(grad_pre, axis=0)
    grad_pre_b = grad_pre.astype(jnp.bfloat16)
    grad_fc1 = weight_grad(saved_three, grad_pre_b)
    grad_norm_two = back_project(grad_pre_b, full_fc1)
    grad_gain_two = jnp.sum(grad_norm_two * normed_two, axis=0)
    grad_shift_two = jnp.sum(grad_norm_two, axis=0)
    grad_middle = upstream + norm_backward(grad_norm_two, normed_two, inv_two, norm2_gain)
    grad_scale_attn = jnp.sum(grad_middle * attn_out, axis=0)
    grad_attn = grad_middle * scale_attn
    grad_proj_bias = jnp.sum(grad_attn, axis=0)
    grad_attn_b = grad_attn.astype(jnp.bfloat16)
    grad_proj = weight_grad(saved_two, grad_attn_b)
    grad_attended = back_project(grad_attn_b, full_proj).astype(jnp.bfloat16)
    grad_att_img = grad_attended.reshape(IMGS, half_len, heads_here, HD)
    recomputed = jnp.exp(scores - log_total)
    probs_b = recomputed.astype(jnp.bfloat16)
    grad_value_all = jnp.einsum(
        "ihqk,iqhe->ikhe", probs_b, grad_att_img, preferred_element_type=jnp.float32
    )
    grad_probs = jnp.einsum(
        "iqhe,ikhe->ihqk", grad_att_img, value_all, preferred_element_type=jnp.float32
    )
    delta = jnp.sum(grad_att_img.astype(jnp.float32) * attended_img.astype(jnp.float32), axis=3)
    grad_scores = recomputed * (grad_probs - jnp.transpose(delta, (0, 2, 1))[..., None])
    grad_scores_b = grad_scores.astype(jnp.bfloat16)
    grad_query = (
        jnp.einsum("ihqk,ikhe->iqhe", grad_scores_b, key_all, preferred_element_type=jnp.float32)
        * factor
    )
    grad_key_all = (
        jnp.einsum("ihqk,iqhe->ikhe", grad_scores_b, query_img, preferred_element_type=jnp.float32)
        * factor
    )
    grad_kv_all = jnp.concatenate([grad_key_all, grad_value_all], axis=3)
    first_part = grad_kv_all[:, :half_len].reshape(count, heads_here * 2 * HD)
    second_part = grad_kv_all[:, half_len:].reshape(count, heads_here * 2 * HD)
    own_part = jnp.where(lower, first_part, second_part)
    sent_part = jnp.where(lower, second_part, first_part)
    grad_kv = own_part + from_partner(sent_part.astype(jnp.bfloat16), "gx", 0).astype(
        sent_part.dtype
    )
    grad_kv = grad_kv.reshape(count, heads_here, 2, HD)
    grad_query = grad_query.reshape(count, heads_here, HD)
    grad_qv_bias = jnp.stack(
        [jnp.sum(grad_query, axis=0), jnp.sum(grad_kv[:, :, 1], axis=0)], axis=1
    ).reshape(heads_here * 2 * HD)
    grad_mixed = (
        jnp.stack([grad_query, grad_kv[:, :, 0], grad_kv[:, :, 1]], axis=2)
        .astype(jnp.bfloat16)
        .reshape(count, heads_here * 3 * HD)
    )
    grad_qkv = weight_grad(saved_one, grad_mixed)
    grad_norm_one = back_project(grad_mixed, full_qkv)
    grad_gain_one = jnp.sum(grad_norm_one * normed_one, axis=0)
    grad_shift_one = jnp.sum(grad_norm_one, axis=0)
    grad_input = grad_middle + norm_backward(grad_norm_one, normed_one, inv_one, norm1_gain)
    grad_qkv, grad_proj, grad_fc1, grad_fc2 = (
        lax.psum_scatter(
            grad_qkv.astype(jnp.bfloat16), "gx", scatter_dimension=0, tiled=True
        ).astype(jnp.float32),
        lax.psum_scatter(
            grad_proj.astype(jnp.bfloat16), "gx", scatter_dimension=0, tiled=True
        ).astype(jnp.float32),
        lax.psum_scatter(
            grad_fc1.astype(jnp.bfloat16), "gx", scatter_dimension=0, tiled=True
        ).astype(jnp.float32),
        lax.psum_scatter(
            grad_fc2.astype(jnp.bfloat16), "gx", scatter_dimension=0, tiled=True
        ).astype(jnp.float32),
    )
    smalls = lax.psum(
        (
            grad_gain_one,
            grad_shift_one,
            grad_qv_bias,
            grad_proj_bias,
            grad_scale_attn,
            grad_gain_two,
            grad_shift_two,
            grad_fc1_bias,
            grad_fc2_bias,
            grad_scale_mlp,
        ),
        "gx",
    )
    return (
        output,
        grad_input,
        smalls[0],
        smalls[1],
        grad_qkv,
        smalls[2],
        grad_proj,
        smalls[3],
        smalls[4],
        smalls[5],
        smalls[6],
        grad_fc1,
        smalls[7],
        grad_fc2,
        smalls[8],
        smalls[9],
    )


def solution(mesh):
    return jax.shard_map(
        on_device,
        mesh=mesh,
        in_specs=(
            P("gx", "gy"),
            P("gx", "gy"),
            P("gy"),
            P("gy"),
            P("gx", "gy"),
            P("gy"),
            P("gx", "gy"),
            P("gy"),
            P("gy"),
            P("gy"),
            P("gy"),
            P("gx", "gy"),
            P("gy"),
            P("gx", "gy"),
            P("gy"),
            P("gy"),
        ),
        out_specs=(
            P("gx", "gy"),
            P("gx", "gy"),
            P("gy"),
            P("gy"),
            P("gx", "gy"),
            P("gy"),
            P("gx", "gy"),
            P("gy"),
            P("gy"),
            P("gy"),
            P("gy"),
            P("gx", "gy"),
            P("gy"),
            P("gx", "gy"),
            P("gy"),
            P("gy"),
        ),
        check_vma=False,
    )
```

profile of v0, /device:TPU:0, one launch (start us, length us, event | category | flops | bytes accessed | tf_op | source)
XLA Modules:
  0.0 869.4 jit_solution(13419016381353141579)
XLA Ops:
  7.2 1.2 convert_reduce_fusion
  8.4 23.4 %all-reduce.3 = (f32[685]{0:T(1024)S(1)}, f32[685]{0:T(1024)S(1)}) all-reduce(f32[685]{0:T(1024)S(1)} %get-tuple-element.31, f32[685]{0:T(1024)S(1)} %get-tuple-element.30), channel_id=1, replica_groups=mesh['gx'=4,'gy'=8] {'gy'}, use_global_device_ids=true, to_apply=%region_3.0 | all-reduce | flops 1370 | bytes 10960 | tf_op jit(solution)/shard_map/psum | solution.py:37
  31.9 0.6 copy-done.20
  32.4 1.9 fusion.33
  34.4 0.8 reshape.185
  35.1 8.8 %all_gather.29 = bf16[1024,384]{1,0:T(8,128)(2,1)S(1)} all-gather(bf16[256,384]{1,0:T(8,128)(2,1)} %param.20), channel_id=1, replica_groups=mesh['gx'=4,'gy'=8] {'gx'}, dimensions={0}, use_global_device_ids=true | all-gather | bytes 983040 | tf_op jit(solution)/shard_map/all_gather | solution.py:94
  43.9 30.4 %all-gather.7.cloned.1.call-done = bf16[685,1024]{1,0:T(8,128)(2,1)} async-done(((bf16[685,128]{1,0:T(8,128)(2,1)}), bf16[685,1024]{1,0:T(8,128)(2,1)}) %all-gather.7.cloned.1.call-update) | async-done | bytes 1402896 | tf_op jit(solution)/shard_map/all_gather | solution.py:52
  74.4 2.2 fusion.66
  76.8 1.7 collective-permute-done
  78.6 1.4 multiply_reduce_fusion
  80.1 1.6 fusion
  81.7 1.5 copy-done
  83.2 2.8 fusion.15
  86.1 0.7 all-gather.17.cloned.1.call-update
  86.8 0.5 all-gather.13.cloned.1.call-update
  87.4 5.8 all_gather.31
  93.2 35.4 %all-gather.9.cloned.1.call-done = bf16[685,1024]{0,1:T(8,128)(2,1)} async-done(((bf16[685,128]{0,1:T(8,128)(2,1)}), bf16[685,1024]{0,1:T(8,128)(2,1)}) %all-gather.9.cloned.1.call-update) | async-done | bytes 1402896 | tf_op jit(solution)/shard_map/all_gather | solution.py:52
  128.6 2.2 fusion.59
  130.8 19.1 %all-reduce.2 = (f32[685]{0:T(1024)S(1)}, f32[685]{0:T(1024)S(1)}) all-reduce(f32[685]{0:T(1024)S(1)} %get-tuple-element.27, f32[685]{0:T(1024)S(1)} %get-tuple-element.26), channel_id=1, replica_groups=mesh['gx'=4,'gy'=8] {'gy'}, use_global_device_ids=true, to_apply=%region_9.10 | all-reduce | flops 1370 | bytes 10960 | tf_op jit(solution)/shard_map/psum | solution.py:37
  149.9 0.9 add_convert_fusion
  150.9 7.1 fusion.45
  158.1 5.3 all-gather.13.cloned.1.call-done
  163.4 45.1 %all-gather.11.cloned.1.call-done = bf16[685,1024]{1,0:T(8,128)(2,1)} async-done(((bf16[685,128]{1,0:T(8,128)(2,1)}), bf16[685,1024]{1,0:T(8,128)(2,1)}) %all-gather.11.cloned.1.call-update) | async-done | bytes 1402896 | tf_op jit(solution)/shard_map/all_gather | solution.py:52
  208.5 191.3 %reduce-scatter.9.cloned.1.call-done = f32[685,512]{1,0:T(8,128)} async-done(((f32[685,4096]{1,0:T(8,128)}), f32[685,512]{1,0:T(8,128)}) %reduce-scatter.9.cloned.1.call-update) | async-done | bytes 1402896 | tf_op jit(solution)/shard_map/reduce_scatter | solution.py:68
  399.8 5.0 fusion.60
  404.9 0.9 copy-done.17
  405.7 2.5 fusion.41
  408.3 0.7 all-gather.15.cloned.1.call-update
  409.1 72.3 %reduce-scatter.11.cloned.1.call-done = f32[685,128]{1,0:T(8,128)} async-done(((f32[685,1024]{1,0:T(8,128)}), f32[685,128]{1,0:T(8,128)}) %reduce-scatter.11.cloned.1.call-update) | async-done | bytes 350736 | tf_op jit(solution)/shard_map/reduce_scatter | solution.py:68
  481.3 2.0 multiply_reduce_fusion.2
  483.3 20.7 %all-reduce.1 = (f32[685]{0:T(1024)S(1)}, f32[685]{0:T(1024)S(1)}) all-reduce(f32[685]{0:T(1024)S(1)} %get-tuple-element.17, f32[685]{0:T(1024)S(1)} %get-tuple-element.21), channel_id=1, replica_groups=mesh['gx'=4,'gy'=8] {'gy'}, use_global_device_ids=true, to_apply=%region_15.16 | all-reduce | flops 1370 | bytes 10960 | tf_op jit(solution)/shard_map/psum | solution.py:46
  504.0 70.5 %all-gather.15.cloned.1.call-done = bf16[685,4096]{1,0:T(8,128)(2,1)} async-done(((bf16[685,512]{1,0:T(8,128)(2,1)}), bf16[685,4096]{1,0:T(8,128)(2,1)}) %all-gather.15.cloned.1.call-update) | async-done | bytes 5611536 | tf_op jit(solution)/shard_map/all_gather | solution.py:52
  574.6 5.6 fusion.26
  580.2 2.1 fusion.47
  582.4 3.4 convolution_convert_fusion.1
  586.0 1.3 convolution_convert_fusion.3
  587.3 0.6 log_add_fusion
  587.9 5.5 convolution_convert_fusion
  593.5 60.7 %reduce-scatter.13.cloned.1.call-done = f32[685,128]{1,0:T(8,128)} async-done(((f32[685,1024]{1,0:T(8,128)}), f32[685,128]{1,0:T(8,128)}) %reduce-scatter.13.cloned.1.call-update) | async-done | bytes 350736 | tf_op jit(solution)/shard_map/reduce_scatter | solution.py:68
  654.2 1.0 convert_element_type.131
  655.3 0.7 copy-done.14
  655.9 0.8 copy.43
  656.7 2.0 copy.44
  658.7 1.1 multiply_reduce_fusion.1
  659.8 6.2 multiply_convert_fusion
  666.1 1.9 fusion.8
  668.0 1.7 fusion.5
  670.8 1.4 fusion.62
  672.4 1.2 copy-done.41
  673.6 2.0 convolution_convert_fusion.2
  675.6 2.5 fusion.67
  678.3 2.2 reduce-scatter.21.cloned.1.call-done
  680.5 1.8 convert_element_type.146
  682.3 20.8 %reduce-scatter.19.cloned.1.call-done = bf16[256,128]{1,0:T(8,128)(2,1)} async-done(((bf16[1024,128]{1,0:T(8,128)(2,1)}), bf16[256,128]{1,0:T(8,128)(2,1)}) %reduce-scatter.19.cloned.1.call-update) | async-done | bytes 65552 | tf_op jit(solution)/shard_map/reduce_scatter | solution.py:210
  703.1 1.5 convert_element_type.144
  704.6 25.7 %reduce-scatter.23.cloned.1.call-done = bf16[1024,128]{1,0:T(8,128)(2,1)} async-done(((bf16[4096,128]{1,0:T(8,128)(2,1)}), bf16[1024,128]{1,0:T(8,128)(2,1)}) %reduce-scatter.23.cloned.1.call-update) | async-done | bytes 262160 | tf_op jit(solution)/shard_map/reduce_scatter | solution.py:216
  730.3 1.8 convert_element_type.148
  732.3 23.8 %reduce-scatter.17.cloned.1.call-done = bf16[256,384]{1,0:T(8,128)(2,1)} async-done(((bf16[1024,384]{1,0:T(8,128)(2,1)}), bf16[256,384]{1,0:T(8,128)(2,1)}) %reduce-scatter.17.cloned.1.call-update) | async-done | bytes 196624 | tf_op jit(solution)/shard_map/reduce_scatter | solution.py:207
  756.1 1.7 convert_element_type.142
  757.8 75.2 %reduce-scatter.15.cloned.1.call-done = f32[685,128]{1,0:T(8,128)} async-done(((f32[685,1024]{1,0:T(8,128)}), f32[685,128]{1,0:T(8,128)}) %reduce-scatter.15.cloned.1.call-update) | async-done | bytes 350736 | tf_op jit(solution)/shard_map/reduce_scatter | solution.py:68
  833.0 1.5 fusion.38
  834.5 19.8 %all-reduce = (f32[685]{0:T(1024)S(1)}, f32[685]{0:T(1024)S(1)}) all-reduce(f32[685]{0:T(1024)S(1)} %get-tuple-element.19, f32[685]{0:T(1024)S(1)} %get-tuple-element.20), channel_id=1, replica_groups=mesh['gx'=4,'gy'=8] {'gy'}, use_global_device_ids=true, to_apply=%region_22.23 | all-reduce | flops 1370 | bytes 10960 | tf_op jit(solution)/shard_map/psum | solution.py:46
  854.4 6.3 all-reduce.4
  860.7 2.2 fusion.37
  (135 shorter events, 2.7 us)
Async XLA Ops:
  7.2 67.2 %all-gather.7.cloned.1.call-start = ((), (), s32[]{:S(2)}) async-start(), calls=%async_computation.8 | async-start | bytes 1585152 | tf_op jit(solution)/shard_map/all_gather | solution.py:52
  31.8 0.6 copy-start.20
  31.8 0.6 copy-start.22
  34.3 94.2 %all-gather.9.cloned.1.call-start = ((), (), s32[]{:S(2)}) async-start(), calls=%async_computation.9 | async-start | bytes 1769472 | tf_op jit(solution)/shard_map/all_gather | solution.py:52
  35.1 43.5 %copy-start.26 = (f32[2,1,64]{2,1,0:T(1,128)}, f32[2,1,64]{2,1,0:T(1,128)S(1)}, u32[]{:S(2)}) copy-start(f32[2,1,64]{2,1,0:T(1,128)S(1)} %get-tuple-element.70) | copy-start | bytes 1540
  43.9 32.8 %copy-start.10 = (bf16[1024,384]{1,0:T(8,128)(2,1)}, bf16[1024,384]{1,0:T(8,128)(2,1)S(1)}, u32[]{:S(2)}) copy-start(bf16[1024,384]{1,0:T(8,128)(2,1)S(1)} %all_gather.29) | copy-start | bytes 2359300
  76.5 3.5 copy-start.13
  76.7 1.8 collective-permute-start
  78.6 3.0 copy-start.1
  78.6 3.0 copy-start.3
  80.1 3.1 copy-start
  83.2 4.2 copy-start.24
  83.2 45.4 %copy-start.6 = (bf16[685,128]{1,0:T(8,128)(2,1)S(1)}, bf16[685,128]{1,0:T(8,128)(2,1)}, u32[]{:S(2)}) copy-start(bf16[685,128]{1,0:T(8,128)(2,1)} %param.16) | copy-start | bytes 526084
  83.2 45.4 %copy-start.28 = (f32[128]{0:T(128)S(1)}, f32[128]{0:T(128)}, u32[]{:S(2)}) copy-start(f32[128]{0:T(128)} %param.24) | copy-start | bytes 1540
  83.2 45.4 %copy-start.35 = (f32[128]{0:T(128)S(1)}, f32[128]{0:T(128)}, u32[]{:S(2)}) copy-start(f32[128]{0:T(128)} %param.23) | copy-start | bytes 1540
  86.0 63.9 %copy-start.34 = (f32[128]{0:T(128)S(1)}, f32[128]{0:T(128)}, u32[]{:S(2)}) copy-start(f32[128]{0:T(128)} %param.25) | copy-start | bytes 1540
  86.0 63.9 %copy-start.40 = (f32[128]{0:T(128)S(1)}, f32[128]{0:T(128)}, u32[]{:S(2)}) copy-start(f32[128]{0:T(128)} %param.26) | copy-start | bytes 1540
  86.0 64.9 %copy-start.19 = (bf16[685,128]{1,0:T(8,128)(2,1)S(1)}, bf16[685,128]{1,0:T(8,128)(2,1)}, u32[]{:S(2)}) copy-start(bf16[685,128]{1,0:T(8,128)(2,1)} %param.17) | copy-start | bytes 526084
  86.0 64.9 %copy-start.30 = (f32[128]{0:T(128)S(1)}, f32[128]{0:T(128)}, u32[]{:S(2)}) copy-start(f32[128]{0:T(128)} %param.31) | copy-start | bytes 1540
  86.0 64.9 %all-gather.17.cloned.1.call-start = ((), (), s32[]{:S(2)}) async-start(), calls=%async_computation.13 | async-start | bytes 1310720 | tf_op jit(solution)/shard_map/all_gather | solution.py:97
  86.7 76.6 %all-gather.13.cloned.1.call-start = ((), (), s32[]{:S(2)}) async-start(), calls=%async_computation.11 | async-start | bytes 1310720 | tf_op jit(solution)/shard_map/all_gather | solution.py:96
  87.3 121.2 %all-gather.11.cloned.1.call-start = ((), (), s32[]{:S(2)}) async-start(), calls=%async_computation.10 | async-start | bytes 1585152 | tf_op jit(solution)/shard_map/all_gather | solution.py:52
  150.8 249.0 %reduce-scatter.9.cloned.1.call-start = ((), (), s32[]{:S(2)}) async-start(), calls=%async_computation.14 | async-start | bytes 12681216 | tf_op jit(solution)/shard_map/reduce_scatter | solution.py:68
  158.0 241.8 %copy-start.42 = (f32[512]{0:T(512)S(1)}, f32[512]{0:T(512)}, u32[]{:S(2)}) copy-start(f32[512]{0:T(512)} %param.28) | copy-start | bytes 6148
  158.1 323.3 %reduce-scatter.11.cloned.1.call-start = ((), (), s32[]{:S(2)}) async-start(), calls=%async_computation.15 | async-start | bytes 3170304 | tf_op jit(solution)/shard_map/reduce_scatter | solution.py:68
  163.4 242.4 %copy-start.15 = (bf16[1024,512]{1,0:T(8,128)(2,1)S(1)}, bf16[1024,512]{1,0:T(8,128)(2,1)}, u32[]{:S(2)}) copy-start(bf16[1024,512]{1,0:T(8,128)(2,1)} %all-gather.13.cloned.1.call-done) | copy-start | bytes 3145732
  404.9 0.9 copy-start.17
  408.2 166.3 %copy-start.16 = (bf16[4096,128]{1,0:T(8,128)(2,1)S(1)}, bf16[4096,128]{1,0:T(8,128)(2,1)}, u32[]{:S(2)}) copy-start(bf16[4096,128]{1,0:T(8,128)(2,1)} %all-gather.17.cloned.1.call-done) | copy-start | bytes 3145732
  408.2 166.3 %copy-start.43 = (f32[128]{0:T(128)S(1)}, f32[128]{0:T(128)}, u32[]{:S(2)}) copy-start(f32[128]{0:T(128)} %param.30) | copy-start | bytes 1540
  408.3 166.3 %all-gather.15.cloned.1.call-start = ((), (), s32[]{:S(2)}) async-start(), calls=%async_computation.12 | async-start | bytes 6340608 | tf_op jit(solution)/shard_map/all_gather | solution.py:52
  409.0 245.2 %reduce-scatter.13.cloned.1.call-start = ((), (), s32[]{:S(2)}) async-start(), calls=%async_computation.16 | async-start | bytes 3170304 | tf_op jit(solution)/shard_map/reduce_scatter | solution.py:68
  580.2 5.7 copy-start.8
  580.2 2.2 copy-start.18
  582.3 3.6 copy-start.5
  582.4 98.2 %reduce-scatter.21.cloned.1.call-start = ((), (), s32[]{:S(2)}) async-start(), calls=%async_computation.20 | async-start | bytes 1310720 | tf_op jit(solution)/shard_map/reduce_scatter | solution.py:213
  585.9 117.2 %reduce-scatter.19.cloned.1.call-start = ((), (), s32[]{:S(2)}) async-start(), calls=%async_computation.19 | async-start | bytes 327680 | tf_op jit(solution)/shard_map/reduce_scatter | solution.py:210
  587.3 143.0 %reduce-scatter.23.cloned.1.call-start = ((), (), s32[]{:S(2)}) async-start(), calls=%async_computation.21 | async-start | bytes 1310720 | tf_op jit(solution)/shard_map/reduce_scatter | solution.py:216
  593.5 162.6 %reduce-scatter.17.cloned.1.call-start = ((), (), s32[]{:S(2)}) async-start(), calls=%async_computation.18 | async-start | bytes 983040 | tf_op jit(solution)/shard_map/reduce_scatter | solution.py:207
  655.3 0.7 copy-start.14
  656.7 11.2 %slice-start = ((s8[7749632]{0:T(1024)(128)(4,1)}), s8[3555328]{0:T(1024)(128)(4,1)S(1)}, s32[]{:S(2)}) async-start(s8[7749632]{0:T(1024)(128)(4,1)} %bitcast.102), calls=%async_computation.22 | async-start | bytes 7110656
  659.8 6.2 copy-start.27
  659.8 8.1 slice-start.1
  666.0 1.9 copy-start.12
  666.1 1.9 copy-start.25
  669.7 1.0 copy-start.2
  669.7 1.1 copy-start.4
  669.9 2.3 collective-permute-start.1
  672.2 1.4 copy-start.41
  672.3 3.3 copy-start.11
  675.6 157.4 %reduce-scatter.15.cloned.1.call-start = ((), (), s32[]{:S(2)}) async-start(), calls=%async_computation.17 | async-start | bytes 3170304 | tf_op jit(solution)/shard_map/reduce_scatter | solution.py:68
  678.1 154.9 %copy-start.7 = (bf16[685,128]{1,0:T(8,128)(2,1)S(1)}, bf16[685,128]{1,0:T(8,128)(2,1)}, u32[]{:S(2)}) copy-start(bf16[685,128]{1,0:T(8,128)(2,1)} %param.16) | copy-start | bytes 526084
  678.1 154.9 %copy-start.21 = (f32[685]{0:T(1024)S(1)}, f32[685]{0:T(1024)}, u32[]{:S(2)}) copy-start(f32[685]{0:T(1024)} %copy-done.20) | copy-start | bytes 8224
  678.2 154.9 %copy-start.23 = (f32[685]{0:T(1024)S(1)}, f32[685]{0:T(1024)}, u32[]{:S(2)}) copy-start(f32[685]{0:T(1024)} %copy-done.22) | copy-start | bytes 8224
  678.2 154.9 %copy-start.29 = (f32[128]{0:T(128)S(1)}, f32[128]{0:T(128)}, u32[]{:S(2)}) copy-start(f32[128]{0:T(128)} %param.18) | copy-start | bytes 1540
  678.2 176.1 %copy-start.31 = (f32[128]{0:T(128)S(1)}, f32[128]{0:T(128)}, u32[]{:S(2)}) copy-start(f32[128]{0:T(128)} %get-tuple-element.16) | copy-start | bytes 1540
  678.2 176.1 %copy-start.32 = (f32[128]{0:T(128)S(1)}, f32[128]{0:T(128)}, u32[]{:S(2)}) copy-start(f32[128]{0:T(128)} %get-tuple-element.22) | copy-start | bytes 1540
  678.2 176.1 %copy-start.33 = (f32[512]{0:T(512)S(1)}, f32[512]{0:T(512)}, u32[]{:S(2)}) copy-start(f32[512]{0:T(512)} %get-tuple-element.50) | copy-start | bytes 6148
  678.2 176.1 %copy-start.36 = (f32[128]{0:T(128)S(1)}, f32[128]{0:T(128)}, u32[]{:S(2)}) copy-start(f32[128]{0:T(128)} %get-tuple-element.28) | copy-start | bytes 1540
  678.2 176.1 %copy-start.37 = (f32[128]{0:T(128)S(1)}, f32[128]{0:T(128)}, u32[]{:S(2)}) copy-start(f32[128]{0:T(128)} %get-tuple-element.29) | copy-start | bytes 1540
  678.2 176.1 %copy-start.38 = (f32[128]{0:T(128)S(1)}, f32[128]{0:T(128)}, u32[]{:S(2)}) copy-start(f32[128]{0:T(128)} %get-tuple-element.62) | copy-start | bytes 1540
  678.2 176.1 %copy-start.39 = (f32[128]{0:T(128)S(1)}, f32[128]{0:T(128)}, u32[]{:S(2)}) copy-start(f32[128]{0:T(128)} %get-tuple-element.63) | copy-start | bytes 1540
  678.2 182.5 %copy-start.9 = (f32[685,128]{1,0:T(8,128)S(1)}, f32[685,128]{1,0:T(8,128)}, u32[]{:S(2)}) copy-start(f32[685,128]{1,0:T(8,128)} %copy-done.8) | copy-start | bytes 1052164
Sparse Core Ops, SparseCore 0:
  34.4 39.8 all-gather.6
  86.1 42.3 all-gather.8
  130.1 15.0 all-gather.16
  146.6 16.6 all-gather.12
  165.8 42.6 all-gather.10
  212.0 187.7 reduce-scatter.8
  408.4 72.9 reduce-scatter.10
  483.4 91.1 all-gather.14
  582.5 71.7 reduce-scatter.12
  656.6 23.8 reduce-scatter.20
  683.0 20.0 reduce-scatter.18
  705.5 24.7 reduce-scatter.22
  732.8 23.2 reduce-scatter.16
  759.5 73.5 reduce-scatter.14
where the time goes:
time: 870 us; the launch traced here: 869 us
  waiting for transfers between devices  663 us (76%)
  blocking collectives  104 us (12%)
  matrix products  56.9 us (7%)
  other arithmetic  21.6 us (2%)
  between operations  14.6 us (2%)
  local copies, waits for them, and re-layouts  9.18 us (1%)
    reduce_scatter x4, waiting for transfers between devices, back_project(): return lax.psum_scatter(term, 'gy', scatter_dimension=1, tiled=True)  400 us
    all_gather x4, waiting for transfers between devices, project(): lax.all_gather(inputs, 'gy', axis=1, tiled=True)  181 us
    psum x2, blocking collectives, norm_forward(): lax.psum((jnp.sum(rows, axis=1), jnp.sum(rows * rows, axis=1)), 'gy')  42.5 us
    psum x2, blocking collectives, norm_backward(): lax.psum((jnp.sum(scaled, axis=1), jnp.sum(scaled * normed, axis=1)), 'gy')  40.4 us
    reduce_scatter x1, waiting for transfers between devices, on_device(): lax.psum_scatter(grad_fc2.astype(jnp.bfloat16), 'gx', scatter_dimension=0...  25.7 us
    reduce_scatter x1, waiting for transfers between devices, on_device(): lax.psum_scatter(grad_qkv.astype(jnp.bfloat16), 'gx', scatter_dimension=0...  23.8 us
    reduce_scatter x1, waiting for transfers between devices, on_device(): lax.psum_scatter(grad_proj.astype(jnp.bfloat16), 'gx', scatter_dimension=...  20.8 us
  transfers between devices with their start and end apart: 16, of which 14 were waited for; matrix products, arithmetic and copies ran while one was open for 6% of the time, Pallas kernels for 0%

commit v1 on v0

--- a/solution.py
+++ b/solution.py
@@ -9,6 +9,13 @@
 EPS = 1e-06
 ROOT_HALF = 0.7071067811865476
 INV_ROOT_TAU = 0.3989422804014327
+
+
+def series_cut(z_in, dim_k):
+    v_now = list(z_in.shape[1:])
+    v_now[dim_k] *= z_in.shape[0]
+    x_new = jnp.moveaxis(z_in, 0, dim_k).reshape(v_now)
+    return x_new
 
 
 def from_partner(block, axis, bit):
@@ -48,9 +55,26 @@
 
 
 def project(inputs, weight):
-    result = jnp.dot(
-        lax.all_gather(inputs, "gy", axis=1, tiled=True), weight, preferred_element_type=jnp.float32
-    )
+
+    def group_chunk(at_axis, along_axis, block_in):
+        nodes = lax.axis_size(along_axis)
+        line_up = list(map(lambda at: (at, (at + 1) % nodes), range(nodes)))
+        cards = [(to_i, idx) for idx, to_i in line_up]
+        right_arr, b_now = ([], [])
+        for d in [*range(nodes - 1)]:
+            if d % 2 == 0:
+                right_arr.append(
+                    lax.ppermute(right_arr[-1] if right_arr else block_in, along_axis, line_up)
+                )
+            else:
+                b_now.append(lax.ppermute(b_now[-1] if b_now else block_in, along_axis, cards))
+        side_arr = jnp.stack([*right_arr[::-1], block_in, *b_now])
+        all_values = lax.axis_index(along_axis) - len(right_arr)
+        side_arr = side_arr[(jnp.arange(nodes) - all_values) % nodes]
+        latest = series_cut(side_arr, at_axis)
+        return latest
+
+    result = jnp.dot(group_chunk(1, "gy", inputs), weight, preferred_element_type=jnp.float32)
     return (result, inputs)
 
 

time: 870 us -> 966 us (1.11)
  starting transfers between devices: 0.71 us -> 73.9 us
  waiting for transfers between devices: 663 us -> 619 us
  local copies, waits for them, and re-layouts: 9.18 us -> 52.8 us
  blocking collectives: 104 us -> 118 us
    reduce_scatter x4, waiting for transfers between devices: 400 us -> 147 us  [back_project(): return lax.psum_scatter(term, 'gy', scatter_dimension=1, tiled=True)]
    ppermute x0 -> x28, waiting for transfers between devices: none -> 212 us  [the longest x16 153 us: group_chunk(): lax.ppermute(right_arr[-1] if right_arr else block_in, along_axis, line_up)]
    ppermute x0 -> x28, starting transfers between devices: none -> 73 us  [the longest x12 66.6 us: group_chunk(): lax.ppermute(b_now[-1] if b_now else block_in, along_axis, cards)]
    all_gather x4, waiting for transfers between devices: 181 us -> 145 us  [weight_grad(): lax.all_gather(saved, 'gy', axis=1, tiled=True)]
    unnamed x92 -> x128, local copies, waits for them, and re-layouts: 5.52 us -> 26.3 us
    all_gather x1, waiting for transfers between devices: 0.02 us -> 20.3 us  [on_device(): lax.all_gather(fc2_weight, 'gx', axis=0, tiled=True)]
    reduce_scatter x1, waiting for transfers between devices: 2.24 us -> 19.3 us  [on_device(): lax.psum_scatter(grad_fc1.astype(jnp.bfloat16), 'gx', scatter_dimension=0...]
    psum x2, blocking collectives: 42.5 us -> 55.2 us  [norm_forward(): lax.psum((jnp.sum(rows, axis=1), jnp.sum(rows * rows, axis=1)), 'gy')]
  transfers between devices with their start and end apart: 16 -> 44, of which waited for: 14 -> 29; matrix products, arithmetic and copies ran while one was open for 6% -> 12% of each run, Pallas kernels for 0% -> 0%
where the time goes in v1:
time: 966 us; the launch traced here: 957 us
  waiting for transfers between devices  619 us (64%)
  blocking collectives  118 us (12%)
  starting transfers between devices  73.9 us (8%)
  matrix products  57.4 us (6%)
  local copies, waits for them, and re-layouts  52.8 us (5%)
  other arithmetic  20.4 us (2%)
  between operations  15.4 us (2%)
    ppermute x16, waiting for transfers between devices, group_chunk(): lax.ppermute(right_arr[-1] if right_arr else block_in, along_axis, line_up)  153 us
    reduce_scatter x4, waiting for transfers between devices, back_project(): return lax.psum_scatter(term, 'gy', scatter_dimension=1, tiled=True)  147 us
    all_gather x4, waiting for transfers between devices, weight_grad(): lax.all_gather(saved, 'gy', axis=1, tiled=True)  145 us
    ppermute x12, starting transfers between devices, group_chunk(): lax.ppermute(b_now[-1] if b_now else block_in, along_axis, cards)  66.6 us
    ppermute x12, waiting for transfers between devices, group_chunk(): lax.ppermute(b_now[-1] if b_now else block_in, along_axis, cards)  58.1 us
    psum x2, blocking collectives, norm_forward(): lax.psum((jnp.sum(rows, axis=1), jnp.sum(rows * rows, axis=1)), 'gy')  55.2 us
    psum x2, blocking collectives, norm_backward(): lax.psum((jnp.sum(scaled, axis=1), jnp.sum(scaled * normed, axis=1)), 'gy')  43.1 us
    unnamed x128, local copies, waits for them, and re-layouts  26.3 us
  transfers between devices with their start and end apart: 44, of which 29 were waited for; matrix products, arithmetic and copies ran while one was open for 12% of the time, Pallas kernels for 0%

profile of v1, /device:TPU:0, one launch (start us, length us, event | category | flops | bytes accessed | tf_op | source)
XLA Modules:
  0.0 956.8 jit_solution(11849151248260421216)
XLA Ops:
  8.7 20.3 %all-gather.9.cloned.1.call-done = bf16[4096,128]{1,0:T(8,128)(2,1)} async-done(((bf16[1024,128]{1,0:T(8,128)(2,1)}), bf16[4096,128]{1,0:T(8,128)(2,1)}) %all-gather.9.cloned.1.call-update) | async-done | bytes 1048592 | tf_op jit(solution)/shard_map/all_gather | solution.py:121
  29.0 7.2 fusion.47
  37.4 21.7 %all-reduce.3 = (f32[685]{0:T(1024)S(1)}, f32[685]{0:T(1024)S(1)}) all-reduce(f32[685]{0:T(1024)S(1)} %get-tuple-element.31, f32[685]{0:T(1024)S(1)} %get-tuple-element.30), channel_id=1, replica_groups=mesh['gx'=4,'gy'=8] {'gy'}, use_global_device_ids=true, to_apply=%region_3.0 | all-reduce | flops 1370 | bytes 10960 | tf_op jit(solution)/shard_map/psum | solution.py:44
  59.5 4.7 collective-permute-start.4
  64.2 8.4 collective-permute-done
  72.6 7.7 all_gather.24
  81.6 3.1 collective-permute-done.1
  84.7 4.8 collective-permute-start.5
  89.5 7.9 collective-permute-done.2
  97.4 4.8 collective-permute-start.6
  102.2 7.7 collective-permute-done.3
  113.4 2.5 fusion.14
  125.8 13.4 %collective-permute-done.8 = bf16[685,128]{0,1:T(8,128)(2,1)S(1)} collective-permute-done((bf16[685,128]{0,1:T(8,128)(2,1)S(1)}, bf16[685,128]{0,1:T(8,128)(2,1)S(1)}, u32[]{:S(2)}, u32[]{:S(2)}) %collective-permute-start.8) | collective-permute-done | bytes 175392 | tf_op jit(solution)/shard_map/ppermute | solution.py:67
  139.2 4.7 collective-permute-start.12
  143.9 9.5 collective-permute-done.9
  153.4 5.8 collective-permute-start.13
  159.2 9.7 %collective-permute-done.10 = bf16[685,128]{0,1:T(8,128)(2,1)S(1)} collective-permute-done((bf16[685,128]{0,1:T(8,128)(2,1)S(1)}, bf16[685,128]{0,1:T(8,128)(2,1)S(1)}, u32[]{:S(2)}, u32[]{:S(2)}) %collective-permute-start.10) | collective-permute-done | bytes 175392 | tf_op jit(solution)/shard_map/ppermute | solution.py:67
  168.9 5.8 all_gather.25
  174.7 11.5 %collective-permute-start.14 = (bf16[685,128]{0,1:T(8,128)(2,1)S(1)}, bf16[685,128]{0,1:T(8,128)(2,1)S(1)}, u32[]{:S(2)}, u32[]{:S(2)}) collective-permute-start(bf16[685,128]{0,1:T(8,128)(2,1)S(1)} %collective-permute-done.13), channel_id=1, source_target_pairs={{1,0},{2,1},{3,2},{4,3},{5,4},{6,5},{7,6},{0,7},{9,8},{10,9},{11,1... | collective-permute-start | bytes 526088 | tf_op jit(solution)/shard_map/ppermute | solution.py:70
  191.1 2.5 collective-permute-done.14
  197.1 33.5 %all-reduce.2 = (f32[685]{0:T(1024)S(1)}, f32[685]{0:T(1024)S(1)}) all-reduce(f32[685]{0:T(1024)S(1)} %get-tuple-element.27, f32[685]{0:T(1024)S(1)} %get-tuple-element.26), channel_id=1, replica_groups=mesh['gx'=4,'gy'=8] {'gy'}, use_global_device_ids=true, to_apply=%region_9.10 | all-reduce | flops 1370 | bytes 10960 | tf_op jit(solution)/shard_map/psum | solution.py:44
  231.1 13.5 %collective-permute-done.15 = bf16[685,128]{1,0:T(8,128)(2,1)S(1)} collective-permute-done((bf16[685,128]{1,0:T(8,128)(2,1)S(1)}, bf16[685,128]{1,0:T(8,128)(2,1)S(1)}, u32[]{:S(2)}, u32[]{:S(2)}) %collective-permute-start.15) | collective-permute-done | bytes 175392 | tf_op jit(solution)/shard_map/ppermute | solution.py:67
  244.6 4.7 collective-permute-start.19
  249.3 9.3 collective-permute-done.16
  259.6 3.7 collective-permute-start.20
  263.3 8.8 collective-permute-done.17
  272.1 4.7 collective-permute-start.21
  276.8 7.3 collective-permute-done.18
  289.9 2.2 gather_fusion.2
  293.2 4.7 fusion.64
  297.9 2.6 fusion.43
  304.4 29.4 %collective-permute-done.22 = bf16[685,512]{1,0:T(8,128)(2,1)S(1)} collective-permute-done((bf16[685,512]{1,0:T(8,128)(2,1)S(1)}, bf16[685,512]{1,0:T(8,128)(2,1)S(1)}, u32[]{:S(2)}, u32[]{:S(2)}) %collective-permute-start.22) | collective-permute-done | bytes 701472 | tf_op jit(solution)/shard_map/ppermute | solution.py:67
  333.8 4.7 collective-permute-start.26
  338.6 25.5 %collective-permute-done.23 = bf16[685,512]{1,0:T(8,128)(2,1)S(1)} collective-permute-done((bf16[685,512]{1,0:T(8,128)(2,1)S(1)}, bf16[685,512]{1,0:T(8,128)(2,1)S(1)}, u32[]{:S(2)}, u32[]{:S(2)}) %collective-permute-start.23) | collective-permute-done | bytes 701472 | tf_op jit(solution)/shard_map/ppermute | solution.py:67
  364.0 2.5 collective-permute-start.24
  366.5 22.1 %collective-permute-done.26 = bf16[685,512]{1,0:T(8,128)(2,1)S(1)} collective-permute-done((bf16[685,512]{1,0:T(8,128)(2,1)S(1)}, bf16[685,512]{1,0:T(8,128)(2,1)S(1)}, u32[]{:S(2)}, u32[]{:S(2)}) %collective-permute-start.26) | collective-permute-done | bytes 701472 | tf_op jit(solution)/shard_map/ppermute | solution.py:70
  388.6 8.5 collective-permute-start.27
  397.2 25.1 %collective-permute-done.27 = bf16[685,512]{1,0:T(8,128)(2,1)S(1)} collective-permute-done((bf16[685,512]{1,0:T(8,128)(2,1)S(1)}, bf16[685,512]{1,0:T(8,128)(2,1)S(1)}, u32[]{:S(2)}, u32[]{:S(2)}) %collective-permute-start.27) | collective-permute-done | bytes 701472 | tf_op jit(solution)/shard_map/ppermute | solution.py:70
  422.3 3.9 collective-permute-start.28
  432.7 8.1 collective-permute-done.28
  441.7 5.9 gather_fusion.3
  447.6 5.9 copy.42
  453.9 6.4 copy.50
  462.2 23.3 %all-reduce.1 = (f32[685]{0:T(1024)S(1)}, f32[685]{0:T(1024)S(1)}) all-reduce(f32[685]{0:T(1024)S(1)} %get-tuple-element.17, f32[685]{0:T(1024)S(1)} %get-tuple-element.21), channel_id=1, replica_groups=mesh['gx'=4,'gy'=8] {'gy'}, use_global_device_ids=true, to_apply=%region_15.16 | all-reduce | flops 1370 | bytes 10960 | tf_op jit(solution)/shard_map/psum | solution.py:53
  485.6 5.6 fusion.28
  491.3 2.2 fusion.49
  494.4 3.4 convolution_convert_fusion.1
  497.9 31.5 %all-gather.13.cloned.1.call-done = bf16[685,1024]{0,1:T(8,128)(2,1)} async-done(((bf16[685,128]{0,1:T(8,128)(2,1)}), bf16[685,1024]{0,1:T(8,128)(2,1)}) %all-gather.13.cloned.1.call-update) | async-done | bytes 1402896 | tf_op jit(solution)/shard_map/all_gather | solution.py:84
  529.4 2.7 convolution_convert_fusion.3
  532.7 88.6 %all-gather.17.cloned.1.call-done = bf16[685,4096]{1,0:T(8,128)(2,1)} async-done(((bf16[685,512]{1,0:T(8,128)(2,1)}), bf16[685,4096]{1,0:T(8,128)(2,1)}) %all-gather.17.cloned.1.call-update) | async-done | bytes 5611536 | tf_op jit(solution)/shard_map/all_gather | solution.py:84
  621.3 5.5 convolution_convert_fusion
  626.9 70.5 %reduce-scatter.13.cloned.1.call-done = f32[685,128]{1,0:T(8,128)} async-done(((f32[685,1024]{1,0:T(8,128)}), f32[685,128]{1,0:T(8,128)}) %reduce-scatter.13.cloned.1.call-update) | async-done | bytes 350736 | tf_op jit(solution)/shard_map/reduce_scatter | solution.py:92
  703.9 5.9 multiply_convert_fusion
  716.4 24.8 %all-gather.11.cloned.1.call-done = bf16[685,1024]{1,0:T(8,128)(2,1)} async-done(((bf16[685,128]{1,0:T(8,128)(2,1)}), bf16[685,1024]{1,0:T(8,128)(2,1)}) %all-gather.11.cloned.1.call-update) | async-done | bytes 1402896 | tf_op jit(solution)/shard_map/all_gather | solution.py:84
  741.2 3.4 convolution_convert_fusion.2
  744.6 2.5 fusion.70
  747.3 19.3 %reduce-scatter.21.cloned.1.call-done = bf16[256,512]{1,0:T(8,128)(2,1)} async-done(((bf16[1024,512]{1,0:T(8,128)(2,1)}), bf16[256,512]{1,0:T(8,128)(2,1)}) %reduce-scatter.21.cloned.1.call-update) | async-done | bytes 262160 | tf_op jit(solution)/shard_map/reduce_scatter | solution.py:237
  768.4 20.8 %reduce-scatter.19.cloned.1.call-done = bf16[256,128]{1,0:T(8,128)(2,1)} async-done(((bf16[1024,128]{1,0:T(8,128)(2,1)}), bf16[256,128]{1,0:T(8,128)(2,1)}) %reduce-scatter.19.cloned.1.call-update) | async-done | bytes 65552 | tf_op jit(solution)/shard_map/reduce_scatter | solution.py:234
  790.8 25.5 %reduce-scatter.23.cloned.1.call-done = bf16[1024,128]{1,0:T(8,128)(2,1)} async-done(((bf16[4096,128]{1,0:T(8,128)(2,1)}), bf16[1024,128]{1,0:T(8,128)(2,1)}) %reduce-scatter.23.cloned.1.call-update) | async-done | bytes 262160 | tf_op jit(solution)/shard_map/reduce_scatter | solution.py:240
  818.1 24.0 %reduce-scatter.17.cloned.1.call-done = bf16[256,384]{1,0:T(8,128)(2,1)} async-done(((bf16[1024,384]{1,0:T(8,128)(2,1)}), bf16[256,384]{1,0:T(8,128)(2,1)}) %reduce-scatter.17.cloned.1.call-update) | async-done | bytes 196624 | tf_op jit(solution)/shard_map/reduce_scatter | solution.py:231
  843.8 76.2 %reduce-scatter.15.cloned.1.call-done = f32[685,128]{1,0:T(8,128)} async-done(((f32[685,1024]{1,0:T(8,128)}), f32[685,128]{1,0:T(8,128)}) %reduce-scatter.15.cloned.1.call-update) | async-done | bytes 350736 | tf_op jit(solution)/shard_map/reduce_scatter | solution.py:92
  921.5 19.8 %all-reduce = (f32[685]{0:T(1024)S(1)}, f32[685]{0:T(1024)S(1)}) all-reduce(f32[685]{0:T(1024)S(1)} %get-tuple-element.19, f32[685]{0:T(1024)S(1)} %get-tuple-element.20), channel_id=1, replica_groups=mesh['gx'=4,'gy'=8] {'gy'}, use_global_device_ids=true, to_apply=%region_22.23 | all-reduce | flops 1370 | bytes 10960 | tf_op jit(solution)/shard_map/psum | solution.py:53
  941.4 6.3 all-reduce.4
  947.7 2.2 fusion.39
  (244 shorter events, 71.0 us)
Async XLA Ops:
  7.2 21.8 %all-gather.9.cloned.1.call-start = ((), (), s32[]{:S(2)}) async-start(), calls=%async_computation.9 | async-start | bytes 1310720 | tf_op jit(solution)/shard_map/all_gather | solution.py:121
  7.9 285.0 %all-gather.7.cloned.1.call-start = ((), (), s32[]{:S(2)}) async-start(), calls=%async_computation.8 | async-start | bytes 1310720 | tf_op jit(solution)/shard_map/all_gather | solution.py:120
  8.7 284.3 %reduce-scatter.9.cloned.1.call-start = ((), (), s32[]{:S(2)}) async-start(), calls=%async_computation.10 | async-start | bytes 12681216 | tf_op jit(solution)/shard_map/reduce_scatter | solution.py:92
  36.2 45.2 %copy-start.39 = (f32[256]{0:T(256)S(1)}, f32[256]{0:T(256)}, u32[]{:S(2)}) copy-start(f32[256]{0:T(256)} %param.21) | copy-start | bytes 3076
  36.3 424.0 %reduce-scatter.11.cloned.1.call-start = ((), (), s32[]{:S(2)}) async-start(), calls=%async_computation.11 | async-start | bytes 3170304 | tf_op jit(solution)/shard_map/reduce_scatter | solution.py:92
  59.1 50.8 %copy-start.21 = (f32[685]{0:T(1024)}, f32[685]{0:T(1024)S(1)}, u32[]{:S(2)}) copy-start(f32[685]{0:T(1024)S(1)} %get-tuple-element.67) | copy-start | bytes 8224
  59.1 50.8 %copy-start.23 = (f32[685]{0:T(1024)}, f32[685]{0:T(1024)S(1)}, u32[]{:S(2)}) copy-start(f32[685]{0:T(1024)S(1)} %get-tuple-element.68) | copy-start | bytes 8224
  59.4 50.5 %copy-start.17 = (bf16[685,128]{1,0:T(8,128)(2,1)}, bf16[685,128]{1,0:T(8,128)(2,1)S(1)}, u32[]{:S(2)}) copy-start(bf16[685,128]{1,0:T(8,128)(2,1)S(1)} %fusion.35) | copy-start | bytes 526084
  59.4 13.1 %collective-permute-start = (bf16[685,128]{1,0:T(8,128)(2,1)S(1)}, bf16[685,128]{1,0:T(8,128)(2,1)S(1)}, u32[]{:S(2)}, u32[]{:S(2)}) collective-permute-start(bf16[685,128]{1,0:T(8,128)(2,1)S(1)} %fusion.35), channel_id=1, source_target_pairs={{0,1},{1,2},{2,3},{3,4},{4,5},{5,6},{6,7},{7,0},{8,9},{9,10},{10,1... | collective-permute-start | bytes 526088 | tf_op jit(solution)/shard_map/ppermute | solution.py:67
  59.5 25.2 %collective-permute-start.4 = (bf16[685,128]{1,0:T(8,128)(2,1)S(1)}, bf16[685,128]{1,0:T(8,128)(2,1)S(1)}, u32[]{:S(2)}, u32[]{:S(2)}) collective-permute-start(bf16[685,128]{1,0:T(8,128)(2,1)S(1)} %fusion.35), channel_id=1, source_target_pairs={{1,0},{2,1},{3,2},{4,3},{5,4},{6,5},{7,6},{0,7},{9,8},{10,9},{11,1... | collective-permute-start | bytes 526088 | tf_op jit(solution)/shard_map/ppermute | solution.py:70
  72.6 12.1 %collective-permute-start.1 = (bf16[685,128]{1,0:T(8,128)(2,1)S(1)}, bf16[685,128]{1,0:T(8,128)(2,1)S(1)}, u32[]{:S(2)}, u32[]{:S(2)}) collective-permute-start(bf16[685,128]{1,0:T(8,128)(2,1)S(1)} %collective-permute-done), channel_id=1, source_target_pairs={{0,1},{1,2},{2,3},{3,4},{4,5},{5,6},{6,7},{7,0},{8,9},{9,10},{10,1... | collective-permute-start | bytes 526088 | tf_op jit(solution)/shard_map/ppermute | solution.py:67
  84.7 12.7 %collective-permute-start.2 = (bf16[685,128]{1,0:T(8,128)(2,1)S(1)}, bf16[685,128]{1,0:T(8,128)(2,1)S(1)}, u32[]{:S(2)}, u32[]{:S(2)}) collective-permute-start(bf16[685,128]{1,0:T(8,128)(2,1)S(1)} %collective-permute-done.1), channel_id=1, source_target_pairs={{0,1},{1,2},{2,3},{3,4},{4,5},{5,6},{6,7},{7,0},{8,9},{9,10},{10,1... | collective-permute-start | bytes 526088 | tf_op jit(solution)/shard_map/ppermute | solution.py:67
  84.7 12.7 %collective-permute-start.5 = (bf16[685,128]{1,0:T(8,128)(2,1)S(1)}, bf16[685,128]{1,0:T(8,128)(2,1)S(1)}, u32[]{:S(2)}, u32[]{:S(2)}) collective-permute-start(bf16[685,128]{1,0:T(8,128)(2,1)S(1)} %collective-permute-done.4), channel_id=1, source_target_pairs={{1,0},{2,1},{3,2},{4,3},{5,4},{6,5},{7,6},{0,7},{9,8},{10,9},{11,1... | collective-permute-start | bytes 526088 | tf_op jit(solution)/shard_map/ppermute | solution.py:70
  97.4 12.5 %collective-permute-start.3 = (bf16[685,128]{1,0:T(8,128)(2,1)S(1)}, bf16[685,128]{1,0:T(8,128)(2,1)S(1)}, u32[]{:S(2)}, u32[]{:S(2)}) collective-permute-start(bf16[685,128]{1,0:T(8,128)(2,1)S(1)} %collective-permute-done.2), channel_id=1, source_target_pairs={{0,1},{1,2},{2,3},{3,4},{4,5},{5,6},{6,7},{7,0},{8,9},{9,10},{10,1... | collective-permute-start | bytes 526088 | tf_op jit(solution)/shard_map/ppermute | solution.py:67
  97.4 13.0 %collective-permute-start.6 = (bf16[685,128]{1,0:T(8,128)(2,1)S(1)}, bf16[685,128]{1,0:T(8,128)(2,1)S(1)}, u32[]{:S(2)}, u32[]{:S(2)}) collective-permute-start(bf16[685,128]{1,0:T(8,128)(2,1)S(1)} %collective-permute-done.5), channel_id=1, source_target_pairs={{1,0},{2,1},{3,2},{4,3},{5,4},{6,5},{7,6},{0,7},{9,8},{10,9},{11,1... | collective-permute-start | bytes 526088 | tf_op jit(solution)/shard_map/ppermute | solution.py:70
  116.1 1.8 collective-permute-start.7
  122.5 46.4 %copy-start.25 = (bf16[256,128]{1,0:T(8,128)(2,1)S(1)}, bf16[256,128]{1,0:T(8,128)(2,1)}, u32[]{:S(2)}) copy-start(bf16[256,128]{1,0:T(8,128)(2,1)} %param.22) | copy-start | bytes 196612
  124.7 69.5 %copy-start.12 = (bf16[2,64,685]{2,1,0:T(8,128)(2,1)}, bf16[2,64,685]{2,1,0:T(8,128)(2,1)S(1)}, u32[]{:S(2)}) copy-start(bf16[2,64,685]{2,1,0:T(8,128)(2,1)S(1)} %fusion.17) | copy-start | bytes 526084
  124.7 14.5 %collective-permute-start.8 = (bf16[685,128]{0,1:T(8,128)(2,1)S(1)}, bf16[685,128]{0,1:T(8,128)(2,1)S(1)}, u32[]{:S(2)}, u32[]{:S(2)}) collective-permute-start(bf16[685,128]{0,1:T(8,128)(2,1)S(1)} %bitcast.203), channel_id=1, source_target_pairs={{0,1},{1,2},{2,3},{3,4},{4,5},{5,6},{6,7},{7,0},{8,9},{9,10},{10,1... | collective-permute-start | bytes 526088 | tf_op jit(solution)/shard_map/ppermute | solution.py:67
  139.2 14.2 %collective-permute-start.9 = (bf16[685,128]{0,1:T(8,128)(2,1)S(1)}, bf16[685,128]{0,1:T(8,128)(2,1)S(1)}, u32[]{:S(2)}, u32[]{:S(2)}) collective-permute-start(bf16[685,128]{0,1:T(8,128)(2,1)S(1)} %collective-permute-done.8), channel_id=1, source_target_pairs={{0,1},{1,2},{2,3},{3,4},{4,5},{5,6},{6,7},{7,0},{8,9},{9,10},{10,1... | collective-permute-start | bytes 526088 | tf_op jit(solution)/shard_map/ppermute | solution.py:67
  139.2 14.2 %collective-permute-start.12 = (bf16[685,128]{0,1:T(8,128)(2,1)S(1)}, bf16[685,128]{0,1:T(8,128)(2,1)S(1)}, u32[]{:S(2)}, u32[]{:S(2)}) collective-permute-start(bf16[685,128]{0,1:T(8,128)(2,1)S(1)} %bitcast.204), channel_id=1, source_target_pairs={{1,0},{2,1},{3,2},{4,3},{5,4},{6,5},{7,6},{0,7},{9,8},{10,9},{11,1... | collective-permute-start | bytes 526088 | tf_op jit(solution)/shard_map/ppermute | solution.py:70
  153.4 15.5 %collective-permute-start.10 = (bf16[685,128]{0,1:T(8,128)(2,1)S(1)}, bf16[685,128]{0,1:T(8,128)(2,1)S(1)}, u32[]{:S(2)}, u32[]{:S(2)}) collective-permute-start(bf16[685,128]{0,1:T(8,128)(2,1)S(1)} %collective-permute-done.9), channel_id=1, source_target_pairs={{0,1},{1,2},{2,3},{3,4},{4,5},{5,6},{6,7},{7,0},{8,9},{9,10},{10,1... | collective-permute-start | bytes 526088 | tf_op jit(solution)/shard_map/ppermute | solution.py:67
  153.4 21.3 %collective-permute-start.13 = (bf16[685,128]{0,1:T(8,128)(2,1)S(1)}, bf16[685,128]{0,1:T(8,128)(2,1)S(1)}, u32[]{:S(2)}, u32[]{:S(2)}) collective-permute-start(bf16[685,128]{0,1:T(8,128)(2,1)S(1)} %collective-permute-done.12), channel_id=1, source_target_pairs={{1,0},{2,1},{3,2},{4,3},{5,4},{6,5},{7,6},{0,7},{9,8},{10,9},{11,1... | collective-permute-start | bytes 526088 | tf_op jit(solution)/shard_map/ppermute | solution.py:70
  168.9 17.3 %collective-permute-start.11 = (bf16[685,128]{0,1:T(8,128)(2,1)S(1)}, bf16[685,128]{0,1:T(8,128)(2,1)S(1)}, u32[]{:S(2)}, u32[]{:S(2)}) collective-permute-start(bf16[685,128]{0,1:T(8,128)(2,1)S(1)} %collective-permute-done.10), channel_id=1, source_target_pairs={{0,1},{1,2},{2,3},{3,4},{4,5},{5,6},{6,7},{7,0},{8,9},{9,10},{10,1... | collective-permute-start | bytes 526088 | tf_op jit(solution)/shard_map/ppermute | solution.py:67
  174.7 18.8 %collective-permute-start.14 = (bf16[685,128]{0,1:T(8,128)(2,1)S(1)}, bf16[685,128]{0,1:T(8,128)(2,1)S(1)}, u32[]{:S(2)}, u32[]{:S(2)}) collective-permute-start(bf16[685,128]{0,1:T(8,128)(2,1)S(1)} %collective-permute-done.13), channel_id=1, source_target_pairs={{1,0},{2,1},{3,2},{4,3},{5,4},{6,5},{7,6},{0,7},{9,8},{10,9},{11,1... | collective-permute-start | bytes 526088 | tf_op jit(solution)/shard_map/ppermute | solution.py:70
  231.0 61.1 %copy-start.18 = (bf16[685,128]{1,0:T(8,128)(2,1)}, bf16[685,128]{1,0:T(8,128)(2,1)S(1)}, u32[]{:S(2)}) copy-start(bf16[685,128]{1,0:T(8,128)(2,1)S(1)} %add_convert_fusion) | copy-start | bytes 526084
  231.0 13.6 %collective-permute-start.15 = (bf16[685,128]{1,0:T(8,128)(2,1)S(1)}, bf16[685,128]{1,0:T(8,128)(2,1)S(1)}, u32[]{:S(2)}, u32[]{:S(2)}) collective-permute-start(bf16[685,128]{1,0:T(8,128)(2,1)S(1)} %add_convert_fusion), channel_id=1, source_target_pairs={{0,1},{1,2},{2,3},{3,4},{4,5},{5,6},{6,7},{7,0},{8,9},{9,10},{10,1... | collective-permute-start | bytes 526088 | tf_op jit(solution)/shard_map/ppermute | solution.py:67
  244.6 14.0 %collective-permute-start.16 = (bf16[685,128]{1,0:T(8,128)(2,1)S(1)}, bf16[685,128]{1,0:T(8,128)(2,1)S(1)}, u32[]{:S(2)}, u32[]{:S(2)}) collective-permute-start(bf16[685,128]{1,0:T(8,128)(2,1)S(1)} %collective-permute-done.15), channel_id=1, source_target_pairs={{0,1},{1,2},{2,3},{3,4},{4,5},{5,6},{6,7},{7,0},{8,9},{9,10},{10,1... | collective-permute-start | bytes 526088 | tf_op jit(solution)/shard_map/ppermute | solution.py:67
  244.6 15.0 %collective-permute-start.19 = (bf16[685,128]{1,0:T(8,128)(2,1)S(1)}, bf16[685,128]{1,0:T(8,128)(2,1)S(1)}, u32[]{:S(2)}, u32[]{:S(2)}) collective-permute-start(bf16[685,128]{1,0:T(8,128)(2,1)S(1)} %add_convert_fusion), channel_id=1, source_target_pairs={{1,0},{2,1},{3,2},{4,3},{5,4},{6,5},{7,6},{0,7},{9,8},{10,9},{11,1... | collective-permute-start | bytes 526088 | tf_op jit(solution)/shard_map/ppermute | solution.py:70
  258.5 13.6 %collective-permute-start.17 = (bf16[685,128]{1,0:T(8,128)(2,1)S(1)}, bf16[685,128]{1,0:T(8,128)(2,1)S(1)}, u32[]{:S(2)}, u32[]{:S(2)}) collective-permute-start(bf16[685,128]{1,0:T(8,128)(2,1)S(1)} %collective-permute-done.16), channel_id=1, source_target_pairs={{0,1},{1,2},{2,3},{3,4},{4,5},{5,6},{6,7},{7,0},{8,9},{9,10},{10,1... | collective-permute-start | bytes 526088 | tf_op jit(solution)/shard_map/ppermute | solution.py:67
  259.6 12.5 %collective-permute-start.20 = (bf16[685,128]{1,0:T(8,128)(2,1)S(1)}, bf16[685,128]{1,0:T(8,128)(2,1)S(1)}, u32[]{:S(2)}, u32[]{:S(2)}) collective-permute-start(bf16[685,128]{1,0:T(8,128)(2,1)S(1)} %collective-permute-done.19), channel_id=1, source_target_pairs={{1,0},{2,1},{3,2},{4,3},{5,4},{6,5},{7,6},{0,7},{9,8},{10,9},{11,1... | collective-permute-start | bytes 526088 | tf_op jit(solution)/shard_map/ppermute | solution.py:70
  272.1 12.1 %collective-permute-start.18 = (bf16[685,128]{1,0:T(8,128)(2,1)S(1)}, bf16[685,128]{1,0:T(8,128)(2,1)S(1)}, u32[]{:S(2)}, u32[]{:S(2)}) collective-permute-start(bf16[685,128]{1,0:T(8,128)(2,1)S(1)} %collective-permute-done.17), channel_id=1, source_target_pairs={{0,1},{1,2},{2,3},{3,4},{4,5},{5,6},{6,7},{7,0},{8,9},{9,10},{10,1... | collective-permute-start | bytes 526088 | tf_op jit(solution)/shard_map/ppermute | solution.py:67
  272.1 17.1 %collective-permute-start.21 = (bf16[685,128]{1,0:T(8,128)(2,1)S(1)}, bf16[685,128]{1,0:T(8,128)(2,1)S(1)}, u32[]{:S(2)}, u32[]{:S(2)}) collective-permute-start(bf16[685,128]{1,0:T(8,128)(2,1)S(1)} %collective-permute-done.20), channel_id=1, source_target_pairs={{1,0},{2,1},{3,2},{4,3},{5,4},{6,5},{7,6},{0,7},{9,8},{10,9},{11,1... | collective-permute-start | bytes 526088 | tf_op jit(solution)/shard_map/ppermute | solution.py:70
  300.5 194.0 %all-gather.15.cloned.1.call-start = ((), (), s32[]{:S(2)}) async-start(), calls=%async_computation.18 | async-start | bytes 1585152 | tf_op jit(solution)/shard_map/all_gather | solution.py:84
  301.1 228.3 %all-gather.13.cloned.1.call-start = ((), (), s32[]{:S(2)}) async-start(), calls=%async_computation.16 | async-start | bytes 1769472 | tf_op jit(solution)/shard_map/all_gather | solution.py:84
  301.6 319.7 %all-gather.17.cloned.1.call-start = ((), (), s32[]{:S(2)}) async-start(), calls=%async_computation.20 | async-start | bytes 6340608 | tf_op jit(solution)/shard_map/all_gather | solution.py:84
  302.4 395.0 %reduce-scatter.13.cloned.1.call-start = ((), (), s32[]{:S(2)}) async-start(), calls=%async_computation.12 | async-start | bytes 3170304 | tf_op jit(solution)/shard_map/reduce_scatter | solution.py:92
  302.4 31.4 %collective-permute-start.22 = (bf16[685,512]{1,0:T(8,128)(2,1)S(1)}, bf16[685,512]{1,0:T(8,128)(2,1)S(1)}, u32[]{:S(2)}, u32[]{:S(2)}) collective-permute-start(bf16[685,512]{1,0:T(8,128)(2,1)S(1)} %copy-done.11), channel_id=1, source_target_pairs={{0,1},{1,2},{2,3},{3,4},{4,5},{5,6},{6,7},{7,0},{8,9},{9,10},{10,1... | collective-permute-start | bytes 2104328 | tf_op jit(solution)/shard_map/ppermute | solution.py:67
  333.8 30.2 %collective-permute-start.23 = (bf16[685,512]{1,0:T(8,128)(2,1)S(1)}, bf16[685,512]{1,0:T(8,128)(2,1)S(1)}, u32[]{:S(2)}, u32[]{:S(2)}) collective-permute-start(bf16[685,512]{1,0:T(8,128)(2,1)S(1)} %collective-permute-done.22), channel_id=1, source_target_pairs={{0,1},{1,2},{2,3},{3,4},{4,5},{5,6},{6,7},{7,0},{8,9},{9,10},{10,1... | collective-permute-start | bytes 2104328 | tf_op jit(solution)/shard_map/ppermute | solution.py:67
  333.8 54.8 %collective-permute-start.26 = (bf16[685,512]{1,0:T(8,128)(2,1)S(1)}, bf16[685,512]{1,0:T(8,128)(2,1)S(1)}, u32[]{:S(2)}, u32[]{:S(2)}) collective-permute-start(bf16[685,512]{1,0:T(8,128)(2,1)S(1)} %copy-done.11), channel_id=1, source_target_pairs={{1,0},{2,1},{3,2},{4,3},{5,4},{6,5},{7,6},{0,7},{9,8},{10,9},{11,1... | collective-permute-start | bytes 2104328 | tf_op jit(solution)/shard_map/ppermute | solution.py:70
  364.0 33.1 %collective-permute-start.24 = (bf16[685,512]{1,0:T(8,128)(2,1)S(1)}, bf16[685,512]{1,0:T(8,128)(2,1)S(1)}, u32[]{:S(2)}, u32[]{:S(2)}) collective-permute-start(bf16[685,512]{1,0:T(8,128)(2,1)S(1)} %collective-permute-done.23), channel_id=1, source_target_pairs={{0,1},{1,2},{2,3},{3,4},{4,5},{5,6},{6,7},{7,0},{8,9},{9,10},{10,1... | collective-permute-start | bytes 2104328 | tf_op jit(solution)/shard_map/ppermute | solution.py:67
  388.6 33.7 %collective-permute-start.27 = (bf16[685,512]{1,0:T(8,128)(2,1)S(1)}, bf16[685,512]{1,0:T(8,128)(2,1)S(1)}, u32[]{:S(2)}, u32[]{:S(2)}) collective-permute-start(bf16[685,512]{1,0:T(8,128)(2,1)S(1)} %collective-permute-done.26), channel_id=1, source_target_pairs={{1,0},{2,1},{3,2},{4,3},{5,4},{6,5},{7,6},{0,7},{9,8},{10,9},{11,1... | collective-permute-start | bytes 2104328 | tf_op jit(solution)/shard_map/ppermute | solution.py:70
  397.2 29.0 %collective-permute-start.25 = (bf16[685,512]{1,0:T(8,128)(2,1)S(1)}, bf16[685,512]{1,0:T(8,128)(2,1)S(1)}, u32[]{:S(2)}, u32[]{:S(2)}) collective-permute-start(bf16[685,512]{1,0:T(8,128)(2,1)S(1)} %collective-permute-done.24), channel_id=1, source_target_pairs={{0,1},{1,2},{2,3},{3,4},{4,5},{5,6},{6,7},{7,0},{8,9},{9,10},{10,1... | collective-permute-start | bytes 2104328 | tf_op jit(solution)/shard_map/ppermute | solution.py:67
  422.3 18.5 %collective-permute-start.28 = (bf16[685,512]{1,0:T(8,128)(2,1)S(1)}, bf16[685,512]{1,0:T(8,128)(2,1)S(1)}, u32[]{:S(2)}, u32[]{:S(2)}) collective-permute-start(bf16[685,512]{1,0:T(8,128)(2,1)S(1)} %collective-permute-done.27), channel_id=1, source_target_pairs={{1,0},{2,1},{3,2},{4,3},{5,4},{6,5},{7,6},{0,7},{9,8},{10,9},{11,1... | collective-permute-start | bytes 2104328 | tf_op jit(solution)/shard_map/ppermute | solution.py:70
  491.2 38.1 %copy-start.9 = (f32[685,128]{1,0:T(8,128)}, f32[685,128]{1,0:T(8,128)S(1)}, u32[]{:S(2)}) copy-start(f32[685,128]{1,0:T(8,128)S(1)} %get-tuple-element.64) | copy-start | bytes 1052164
  493.4 247.7 %all-gather.11.cloned.1.call-start = ((), (), s32[]{:S(2)}) async-start(), calls=%async_computation.14 | async-start | bytes 1585152 | tf_op jit(solution)/shard_map/all_gather | solution.py:84
  494.2 272.4 %reduce-scatter.21.cloned.1.call-start = ((), (), s32[]{:S(2)}) async-start(), calls=%async_computation.19 | async-start | bytes 1310720 | tf_op jit(solution)/shard_map/reduce_scatter | solution.py:237
  497.8 291.3 %reduce-scatter.19.cloned.1.call-start = ((), (), s32[]{:S(2)}) async-start(), calls=%async_computation.17 | async-start | bytes 327680 | tf_op jit(solution)/shard_map/reduce_scatter | solution.py:234
  532.1 284.2 %reduce-scatter.23.cloned.1.call-start = ((), (), s32[]{:S(2)}) async-start(), calls=%async_computation.21 | async-start | bytes 1310720 | tf_op jit(solution)/shard_map/reduce_scatter | solution.py:240
  626.9 215.2 %reduce-scatter.17.cloned.1.call-start = ((), (), s32[]{:S(2)}) async-start(), calls=%async_computation.15 | async-start | bytes 983040 | tf_op jit(solution)/shard_map/reduce_scatter | solution.py:231
  713.7 2.5 collective-permute-start.29
  744.5 175.5 %reduce-scatter.15.cloned.1.call-start = ((), (), s32[]{:S(2)}) async-start(), calls=%async_computation.13 | async-start | bytes 3170304 | tf_op jit(solution)/shard_map/reduce_scatter | solution.py:92
  747.1 172.9 %copy-start.4 = (bf16[685,128]{1,0:T(8,128)(2,1)S(1)}, bf16[685,128]{1,0:T(8,128)(2,1)}, u32[]{:S(2)}) copy-start(bf16[685,128]{1,0:T(8,128)(2,1)} %param.16) | copy-start | bytes 526084
  747.1 172.9 %copy-start.22 = (f32[685]{0:T(1024)S(1)}, f32[685]{0:T(1024)}, u32[]{:S(2)}) copy-start(f32[685]{0:T(1024)} %copy-done.21) | copy-start | bytes 8224
  747.2 172.9 %copy-start.24 = (f32[685]{0:T(1024)S(1)}, f32[685]{0:T(1024)}, u32[]{:S(2)}) copy-start(f32[685]{0:T(1024)} %copy-done.23) | copy-start | bytes 8224
  747.2 172.9 %copy-start.30 = (f32[128]{0:T(128)S(1)}, f32[128]{0:T(128)}, u32[]{:S(2)}) copy-start(f32[128]{0:T(128)} %param.18) | copy-start | bytes 1540
  747.2 194.1 %copy-start.35 = (f32[128]{0:T(128)S(1)}, f32[128]{0:T(128)}, u32[]{:S(2)}) copy-start(f32[128]{0:T(128)} %get-tuple-element.16) | copy-start | bytes 1540
  747.2 194.1 %copy-start.36 = (f32[128]{0:T(128)S(1)}, f32[128]{0:T(128)}, u32[]{:S(2)}) copy-start(f32[128]{0:T(128)} %get-tuple-element.22) | copy-start | bytes 1540
  747.2 194.1 %copy-start.37 = (f32[512]{0:T(512)S(1)}, f32[512]{0:T(512)}, u32[]{:S(2)}) copy-start(f32[512]{0:T(512)} %get-tuple-element.50) | copy-start | bytes 6148
  747.2 194.1 %copy-start.41 = (f32[128]{0:T(128)S(1)}, f32[128]{0:T(128)}, u32[]{:S(2)}) copy-start(f32[128]{0:T(128)} %get-tuple-element.28) | copy-start | bytes 1540
  747.2 194.1 %copy-start.42 = (f32[128]{0:T(128)S(1)}, f32[128]{0:T(128)}, u32[]{:S(2)}) copy-start(f32[128]{0:T(128)} %get-tuple-element.29) | copy-start | bytes 1540
  747.2 194.1 %copy-start.43 = (f32[128]{0:T(128)S(1)}, f32[128]{0:T(128)}, u32[]{:S(2)}) copy-start(f32[128]{0:T(128)} %get-tuple-element.62) | copy-start | bytes 1540
  747.3 194.1 %copy-start.44 = (f32[128]{0:T(128)S(1)}, f32[128]{0:T(128)}, u32[]{:S(2)}) copy-start(f32[128]{0:T(128)} %get-tuple-element.63) | copy-start | bytes 1540
  747.3 200.4 %copy-start.10 = (f32[685,128]{1,0:T(8,128)S(1)}, f32[685,128]{1,0:T(8,128)}, u32[]{:S(2)}) copy-start(f32[685,128]{1,0:T(8,128)} %copy-done.9) | copy-start | bytes 1052164
  (29 other events, 396.4 us)
Sparse Core Ops, SparseCore 0:
  9.5 19.4 all-gather.8
  30.6 16.6 all-gather.6
  51.0 240.5 reduce-scatter.8
  300.6 131.7 reduce-scatter.10
  434.8 49.9 all-gather.14
  486.9 42.3 all-gather.12
  531.4 89.8 all-gather.16
  624.8 72.4 reduce-scatter.12
  699.4 41.6 all-gather.10
  743.5 22.9 reduce-scatter.20
  769.0 20.0 reduce-scatter.18
  791.5 24.7 reduce-scatter.22
  818.9 23.1 reduce-scatter.16
  845.5 74.5 reduce-scatter.14
